TPU v7x, 512 devices: a whole 4x8x8 slice. The times are simulated.
512 devices in a mesh: gx: 16 (over y, core), gy: 32 (over z, x).
Axes of the slice: x: 4, y: 8, z: 8, core: 2. Of those that a mesh axis runs over, the one named last changes fastest.
Arguments:
- inputs: bfloat16 [256, 4, 2304], P('gy', None, 'gx'), may hold values from -8 to 8
- cache_pool: bfloat16 [2, 64, 4096, 1024], P(None, 'gx', 'gy'), may hold values from -6 to 6
- lengths: int32 [32], P('gy'), may hold values from 1 to 32768, as said below
- block_table: int32 [32, 33], P('gy'), may hold values from -1 to 63, as said below
- parents: int32 [3, 256], P(None, 'gy'), may hold values from 0 to 7
- norm_gains: float32 [4, 2304], P(None, 'gx'), may hold values from -0.5 to 1
- w_query: bfloat16 [2304, 2048], P('gx', 'gy'), may hold values from -0.125 to 0.125
- w_key: bfloat16 [2304, 1024], P('gx', 'gy'), may hold values from -0.125 to 0.125
- w_value: bfloat16 [2304, 1024], P('gx', 'gy'), may hold values from -0.125 to 0.125
- w_out: bfloat16 [2048, 2304], P('gy', 'gx'), may hold values from -1 to 1
- w_gate: bfloat16 [2304, 9216], P('gx', 'gy'), may hold values from -0.125 to 0.125
- w_up: bfloat16 [2304, 9216], P('gx', 'gy'), may hold values from -0.125 to 0.125
- w_down: bfloat16 [9216, 2304], P('gy', 'gx'), may hold values from -1 to 1
Outputs:
- outputs: bfloat16 [256, 4, 2304], P('gy', None, 'gx')
Inputs may be any that keep to these rules, and one draw needn't show every extreme that they name: `lengths`: a group's beams share its prompt length. block_table[g, j] is the slot, numbered over the index of gy that holds group g as gx index times 4 plus the device's slot, of page first(g) + j of the group, for j up to (lengths[g] - 1) // 128 - first(g), and -1 beyond; no slot is named twice; a device holds at most 4 pages, and some device holds 4. Beam b at step s + 1 continues beam parents[s, b] of its own group, numbered within the group.
All inputs are finite; a program needn't handle non-finite values.
Results may differ from a plain program's by a relative error of at most 0.015.
Values may be sent and summed in bfloat16 or wider, within the bound.
A program may use at most 64 MiB of HBM per device.

v0:
```python
import jax
import jax.numpy as jnp
from jax import lax
from jax.sharding import PartitionSpec as P

D = 2304
HEADS = 8
KV_HEADS = 4
HEAD_DIM = 256
WINDOW = 4096
PAGE = 128
BEAM = 8
EPSILON = 1e-06
SOFT_CAP = 50.0
ROPE_BASE = 10000.0


def rotate(values, positions):
    half_width = values.shape[-1] // 2
    inverse_freq = ROPE_BASE ** (
        -jnp.arange(half_width, dtype=jnp.float32) * 2.0 / values.shape[-1]
    )
    angles = positions[..., None].astype(jnp.float32) * inverse_freq
    cosine = jnp.cos(angles)[..., None, :]
    sine_part = jnp.sin(angles)[..., None, :]
    first_half = values[..., :half_width]
    second_half = values[..., half_width:]
    return jnp.concatenate(
        [
            first_half * cosine - second_half * sine_part,
            second_half * cosine + first_half * sine_part,
        ],
        axis=-1,
    )


def ancestry(parents, beam_count, group_size, steps_count):
    beam_ids = jnp.arange(beam_count, dtype=jnp.int32)
    group_base = beam_ids // group_size * group_size
    table_rows = []
    for moment in range(steps_count):
        current = beam_ids
        chain_list = [beam_ids] * steps_count
        for earlier in range(moment, 0, -1):
            current = group_base + jnp.take(parents[earlier - 1], current)
            chain_list[earlier - 1] = current
        table_rows.append(jnp.stack(chain_list))
    return jnp.stack(table_rows)


def tail_terms(grouped, key_steps, value_steps, ancestors):
    steps_count = grouped.shape[1]
    step_ids = jnp.arange(steps_count, dtype=jnp.int32)
    tail_keys = key_steps[ancestors, step_ids[None, :, None]]
    tail_values = value_steps[ancestors, step_ids[None, :, None]]
    scores = jnp.einsum(
        "bskgd,sjbkd->bskgj", grouped, tail_keys, preferred_element_type=jnp.float32
    )
    allowed = step_ids[None, :] <= step_ids[:, None]
    weights = jnp.where(
        allowed[None, :, None, None, :], jnp.exp(SOFT_CAP * jnp.tanh(scores / SOFT_CAP)), 0.0
    )
    numerator = jnp.einsum(
        "bskgj,sjbkd->bskgd",
        weights.astype(jnp.bfloat16),
        tail_values,
        preferred_element_type=jnp.float32,
    )
    return (numerator, jnp.sum(weights, axis=-1))


def body(
    inputs,
    cache_pool,
    lengths,
    block_table,
    parents,
    norm_gains,
    w_query,
    w_key,
    w_value,
    w_out,
    w_gate,
    w_up,
    w_down,
):
    col_beams, steps_count, width_part = inputs.shape
    group_count = lengths.shape[0]
    slot_count = cache_pool.shape[1]
    rep_heads = HEADS // KV_HEADS
    x_wide = inputs.astype(jnp.float32)
    gain_rows = 1.0 + norm_gains
    square_sum = lax.psum(jnp.sum(x_wide * x_wide, axis=-1), "gx")
    normed_share = (x_wide * lax.rsqrt(square_sum / D + EPSILON)[..., None] * gain_rows[0]).astype(
        jnp.bfloat16
    )
    normed = lax.all_gather(normed_share, "gy", axis=0, tiled=True)
    all_beams = normed.shape[0]
    flat_rows = normed.reshape(-1, width_part)

    def project(weight):
        return jnp.dot(flat_rows, weight, preferred_element_type=jnp.float32).reshape(
            all_beams, steps_count, weight.shape[1]
        )

    query_sum, key_sum, value_sum = lax.psum(
        (project(w_query), project(w_key), project(w_value)), "gx"
    )
    query_raw, key_raw, value_raw = (
        lax.all_to_all(query_sum, "gy", split_axis=0, concat_axis=2, tiled=True),
        lax.all_to_all(key_sum, "gy", split_axis=0, concat_axis=2, tiled=True),
        lax.all_to_all(value_sum, "gy", split_axis=0, concat_axis=2, tiled=True),
    )
    beam_lengths = jnp.repeat(lengths, BEAM)
    step_ids = jnp.arange(steps_count, dtype=jnp.int32)
    positions = beam_lengths[:, None] + step_ids[None, :]
    queries = (
        rotate(query_raw.reshape(col_beams, steps_count, HEADS, HEAD_DIM), positions)
        * HEAD_DIM ** (-0.5)
    ).astype(jnp.bfloat16)
    key_steps = rotate(
        key_raw.reshape(col_beams, steps_count, KV_HEADS, HEAD_DIM), positions
    ).astype(jnp.bfloat16)
    value_steps = value_raw.reshape(col_beams, steps_count, KV_HEADS, HEAD_DIM).astype(jnp.bfloat16)
    grouped = queries.reshape(col_beams, steps_count, KV_HEADS, rep_heads, HEAD_DIM)
    slot_ids = lax.axis_index("gx") * slot_count + jnp.arange(slot_count, dtype=jnp.int32)
    matches = block_table[:, :, None] == slot_ids[None, None, :]
    owner_mask = jnp.any(matches, axis=1)
    slot_used = jnp.any(owner_mask, axis=0)
    page_number = jnp.sum(
        jnp.where(matches, jnp.arange(block_table.shape[1], dtype=jnp.int32)[None, :, None], 0),
        axis=(0, 1),
    )
    first_page = jnp.maximum(lengths - WINDOW + 1, 0) // PAGE
    slot_first = jnp.sum(jnp.where(owner_mask, first_page[:, None], 0), axis=0)
    slot_length = jnp.sum(jnp.where(owner_mask, lengths[:, None], 0), axis=0)
    key_positions = (slot_first + page_number)[:, None] * PAGE + jnp.arange(PAGE, dtype=jnp.int32)[
        None, :
    ]
    group_queries = grouped.reshape(group_count, BEAM, steps_count, KV_HEADS, rep_heads, HEAD_DIM)
    slot_queries = jnp.einsum(
        "an,abskgd->nbskgd",
        owner_mask.astype(jnp.bfloat16),
        group_queries,
        preferred_element_type=jnp.float32,
    ).astype(jnp.bfloat16)
    page_keys = cache_pool[0].reshape(slot_count, PAGE, KV_HEADS, HEAD_DIM)
    page_values = cache_pool[1].reshape(slot_count, PAGE, KV_HEADS, HEAD_DIM)
    scores = jnp.einsum(
        "nbskgd,ntkd->nbskgt", slot_queries, page_keys, preferred_element_type=jnp.float32
    )
    lower_bound = slot_length[:, None] + step_ids[None, :] - WINDOW + 1
    visible = (
        slot_used[:, None, None]
        & (key_positions[:, None, :] < slot_length[:, None, None])
        & (key_positions[:, None, :] >= lower_bound[:, :, None])
    )
    weights = jnp.where(
        visible[:, None, :, None, None, :], jnp.exp(SOFT_CAP * jnp.tanh(scores / SOFT_CAP)), 0.0
    )
    page_den = jnp.sum(weights, axis=-1)
    page_num = jnp.einsum(
        "nbskgt,ntkd->nbskgd",
        weights.astype(jnp.bfloat16),
        page_values,
        preferred_element_type=jnp.float32,
    )
    owner_wide = owner_mask.astype(jnp.float32)
    group_num = jnp.sum(owner_wide[:, :, None, None, None, None, None] * page_num[None], axis=1)
    group_den = jnp.sum(owner_wide[:, :, None, None, None, None] * page_den[None], axis=1)
    total_num, total_den = lax.psum((group_num, group_den), "gx")
    ancestors = ancestry(parents, col_beams, BEAM, steps_count)
    tail_num, tail_den = tail_terms(grouped, key_steps, value_steps, ancestors)
    numerator = total_num.reshape(col_beams, steps_count, KV_HEADS, rep_heads, HEAD_DIM) + tail_num
    denominator = total_den.reshape(col_beams, steps_count, KV_HEADS, rep_heads) + tail_den
    attended = (
        (numerator / denominator[..., None])
        .astype(jnp.bfloat16)
        .reshape(col_beams, steps_count, HEADS * HEAD_DIM)
    )
    head_rows = lax.all_to_all(attended, "gy", split_axis=2, concat_axis=0, tiled=True)
    head_width = head_rows.shape[2]
    attn_part = jnp.dot(
        head_rows.reshape(-1, head_width), w_out, preferred_element_type=jnp.float32
    ).reshape(all_beams, steps_count, width_part)
    attn_full = lax.psum(attn_part, "gy")
    residual = lax.all_gather(inputs, "gy", axis=0, tiled=True).astype(jnp.float32)
    attn_square = lax.psum(jnp.sum(attn_full * attn_full, axis=-1), "gx")
    mixed_full = (
        residual + attn_full * lax.rsqrt(attn_square / D + EPSILON)[..., None] * gain_rows[1]
    )
    mixed_square = lax.psum(jnp.sum(mixed_full * mixed_full, axis=-1), "gx")
    ff_input = (
        mixed_full * lax.rsqrt(mixed_square / D + EPSILON)[..., None] * gain_rows[2]
    ).astype(jnp.bfloat16)
    mixed_rows = lax.dynamic_slice_in_dim(
        mixed_full, lax.axis_index("gy") * col_beams, col_beams, 0
    )
    gate_width = w_gate.shape[1]
    matrix_rows = ff_input.reshape(-1, width_part)
    gate_and_up = jnp.concatenate(
        [
            jnp.dot(matrix_rows, w_gate, preferred_element_type=jnp.float32),
            jnp.dot(matrix_rows, w_up, preferred_element_type=jnp.float32),
        ],
        axis=1,
    )
    activate_gate_and_up = lax.psum_scatter(
        gate_and_up.reshape(ff_input.shape[0], steps_count, 2 * gate_width),
        "gx",
        scatter_dimension=0,
        tiled=True,
    )
    hidden_share = (
        jax.nn.gelu(activate_gate_and_up[..., :gate_width], approximate=True)
        * activate_gate_and_up[..., gate_width:]
    ).astype(jnp.bfloat16)
    hidden_rows = lax.all_gather(hidden_share, "gx", axis=0, tiled=True)
    down_part = jnp.dot(
        hidden_rows.reshape(-1, gate_width), w_down, preferred_element_type=jnp.float32
    ).reshape(hidden_rows.shape[0], steps_count, width_part)
    down_own = lax.psum_scatter(down_part, "gy", scatter_dimension=0, tiled=True)
    out_square = lax.psum(jnp.sum(down_own * down_own, axis=-1), "gx")
    return (
        mixed_rows + down_own * lax.rsqrt(out_square / D + EPSILON)[..., None] * gain_rows[3]
    ).astype(jnp.bfloat16)


def solution(mesh):
    return jax.shard_map(
        body,
        mesh=mesh,
        in_specs=(
            P("gy", None, "gx"),
            P(None, "gx", "gy", None),
            P("gy"),
            P("gy", None),
            P(None, "gy"),
            P(None, "gx"),
            P("gx", "gy"),
            P("gx", "gy"),
            P("gx", "gy"),
            P("gy", "gx"),
            P("gx", "gy"),
            P("gx", "gy"),
            P("gy", "gx"),
        ),
        out_specs=P("gy", None, "gx"),
        check_vma=False,
    )
```

profile of v0, /device:TPU:1, one launch (start us, length us, event | category | flops | bytes accessed | tf_op | source)
XLA Modules:
  0.0 937.1 jit_solution(2836527621570253802)
XLA Ops:
  8.1 29.8 %psum.70 = f32[8,4]{0,1:T(4,128)S(1)} all-reduce(f32[8,4]{0,1:T(4,128)S(1)} %fusion.33), channel_id=1, replica_groups=mesh['gx'=16,'gy'=32] {'gx'}, use_global_device_ids=true, to_apply=%region_3.0 | all-reduce | flops 32 | bytes 256 | tf_op jit(solution)/shard_map/psum | solution.py:93
  38.6 36.1 %all_gather.10 = bf16[256,4,144]{2,0,1:T(8,128)(2,1)S(1)} all-gather(bf16[8,4,144]{2,0,1:T(8,128)(2,1)S(1)} %fusion.35), channel_id=1, replica_groups=mesh['gx'=16,'gy'=32] {'gy'}, dimensions={0}, use_global_device_ids=true | all-gather | bytes 304128 | tf_op jit(solution)/shard_map/all_gather | solution.py:97
  74.7 1.7 fusion.37
  79.1 1.8 fusion.65
  84.6 111.0 %all-reduce.9.cloned.1.call-done = f32[256,4,64]{0,2,1:T(8,128)} async-done(((f32[256,4,64]{0,2,1:T(8,128)}), f32[256,4,64]{0,2,1:T(8,128)}) %all-reduce.9.cloned.1.call-update) | async-done | bytes 262160 | tf_op jit(solution)/shard_map/psum | solution.py:106
  195.6 1.2 copy.204
  196.8 1.2 reshape.614
  198.0 9.9 %all-to-all-start = ((f32[32,1,2048]{2,1,0:T(1,128)}), f32[32,1,2048]{2,1,0:T(1,128)S(1)}, u32[]{:S(2)}, u32[]{:S(2)}) async-start(f32[32,1,2048]{2,1,0:T(1,128)} %reshape.614), calls=%async_computation | async-start | bytes 524288 | tf_op jit(solution)/shard_map/all_to_all | solution.py:110
  208.5 1.3 copy.253
  210.7 0.9 fusion.44
  211.6 7.5 all-to-all-done
  219.6 1.3 reduce.5
  221.9 1.7 fusion.67
  225.1 47.4 %all-reduce.16 = (bf16[256,4,32]{0,2,1:T(8,128)(2,1)S(1)}, f32[8,4,4,2]{0,2,3,1:T(4,128)S(1)}) all-reduce(f32[256,4,32]{0,2,1:T(8,128)S(1)} %fusion.42, f32[8,4,4,2]{0,2,3,1:T(4,128)S(1)} %copy.223), channel_id=1, replica_groups=mesh['gx'=16,'gy'=32] {'gx'}, use_global_device_ids=true, to_apply=%region_8.10 | all-reduce | flops 33024 | bytes 198656 | tf_op jit(solution)/shard_map/psum | solution.py:106
  272.6 0.8 reshape.616
  273.5 3.8 all-to-all-start.2
  278.1 120.2 %all-reduce.15.cloned.1.call-done = (f32[8,4,4,2,256]{4,3,2,1,0:T(2,128)}, f32[256,4,32]{0,2,1:T(8,128)}) async-done(((f32[8,4,4,2,256]{4,3,2,1,0:T(2,128)}, f32[256,4,32]{0,2,1:T(8,128)}), (f32[8,4,4,2,256]{4,3,2,1,0:T(2,128)}, f32[256,4,32]{0,2,1:T(8,128)})) %all-reduce.15.cloned.1.call-update) | async-done | bytes 393232 | tf_op jit(solution)/shard_map/psum | solution.py:171
  398.3 1.1 copy.213
  399.4 1.0 reshape.618
  400.4 9.9 %all-to-all-start.1 = ((f32[32,1,1024]{2,1,0:T(1,128)}), f32[32,1,1024]{2,1,0:T(1,128)S(1)}, u32[]{:S(2)}, u32[]{:S(2)}) async-start(f32[32,1,1024]{2,1,0:T(1,128)} %reshape.618), calls=%async_computation.1 | async-start | bytes 262144 | tf_op jit(solution)/shard_map/all_to_all | solution.py:111
  411.2 1.0 gather_fusion.1
  412.2 7.5 all-to-all-done.1
  419.7 1.0 reduce.6
  421.4 1.0 gather_fusion
  423.7 1.3 copy.250
  425.0 2.3 reshape.620
  427.3 12.7 %all_to_all.54 = bf16[32,2,1024]{2,1,0:T(2,128)(2,1)S(1)} all-to-all(bf16[32,2,1024]{2,1,0:T(2,128)(2,1)S(1)} %reshape.620), channel_id=1, replica_groups=mesh['gx'=16,'gy'=32] {'gy'}, dimensions={0} | all-to-all | bytes 262144 | tf_op jit(solution)/shard_map/all_to_all | solution.py:181
  440.0 2.4 reshape.621
  442.5 2.1 copy.252
  444.6 1.3 fusion.16
  446.0 37.6 %all_gather.9 = bf16[256,4,144]{2,1,0:T(4,128)(2,1)S(1)} all-gather(bf16[8,4,144]{2,1,0:T(4,128)(2,1)S(1)} %copy-done.2), channel_id=1, replica_groups=mesh['gx'=16,'gy'=32] {'gy'}, dimensions={0}, use_global_device_ids=true | all-gather | bytes 304128 | tf_op jit(solution)/shard_map/all_gather | solution.py:187
  483.6 115.7 %all-reduce.11.cloned.1.call-done = f32[256,4,144]{2,0,1:T(8,128)} async-done(((f32[256,4,144]{2,0,1:T(8,128)}), f32[256,4,144]{2,0,1:T(8,128)}) %all-reduce.11.cloned.1.call-update) | async-done | bytes 589840 | tf_op jit(solution)/shard_map/psum | solution.py:186
  599.3 1.4 multiply_reduce_fusion.1
  600.8 28.1 %psum.77 = f32[256,4]{0,1:T(4,128)S(1)} all-reduce(f32[256,4]{0,1:T(4,128)S(1)} %multiply_reduce_fusion.1), channel_id=1, replica_groups=mesh['gx'=16,'gy'=32] {'gx'}, use_global_device_ids=true, to_apply=%region_15.17 | all-reduce | flops 1024 | bytes 8192 | tf_op jit(solution)/shard_map/psum | solution.py:188
  628.9 1.6 multiply_reduce_fusion
  630.5 23.6 %psum.78 = f32[256,4]{0,1:T(4,128)S(1)} all-reduce(f32[256,4]{0,1:T(4,128)S(1)} %get-tuple-element.12), channel_id=1, replica_groups=mesh['gx'=16,'gy'=32] {'gx'}, use_global_device_ids=true, to_apply=%region_17.19 | all-reduce | flops 1024 | bytes 8192 | tf_op jit(solution)/shard_map/psum | solution.py:192
  655.9 1.6 pad_maximum_fusion
  657.4 2.1 copy.232
  659.5 1.9 reshape.525
  661.5 3.4 copy.233
  665.0 57.8 %reduce-scatter.2.cloned.1.call-done = f32[16,4,576]{2,0,1:T(8,128)} async-done(((f32[256,4,576]{2,0,1:T(8,128)}), f32[16,4,576]{2,0,1:T(8,128)}) %reduce-scatter.2.cloned.1.call-update) | async-done | bytes 147472 | tf_op jit(solution)/shard_map/reduce_scatter | solution.py:208
  722.8 1.1 fusion.31
  723.8 19.0 %all_gather.11 = bf16[256,4,288]{2,0,1:T(8,128)(2,1)S(1)} all-gather(bf16[16,4,288]{2,0,1:T(8,128)(2,1)S(1)} %fusion.31), channel_id=1, replica_groups=mesh['gx'=16,'gy'=32] {'gx'}, dimensions={0}, use_global_device_ids=true | all-gather | bytes 626688 | tf_op jit(solution)/shard_map/all_gather | solution.py:218
  743.3 1.7 copy.234
  745.0 1.3 dynamic-slice
  746.9 153.2 %all-reduce.13.cloned.1.call-done = f32[256,4,144]{2,1,0:T(4,128)} async-done(((f32[256,4,144]{2,1,0:T(4,128)}), f32[256,4,144]{2,1,0:T(4,128)}) %all-reduce.13.cloned.1.call-update) | async-done | bytes 589840
  900.1 0.8 multiply_reduce_fusion.3
  901.0 28.1 %psum.79 = f32[8,4]{0,1:T(4,128)S(1)} all-reduce(f32[8,4]{0,1:T(4,128)S(1)} %copy.235), channel_id=1, replica_groups=mesh['gx'=16,'gy'=32] {'gx'}, use_global_device_ids=true, to_apply=%region_21.23 | all-reduce | flops 32 | bytes 256 | tf_op jit(solution)/shard_map/psum | solution.py:223
  (112 shorter events, 19.8 us)
Async XLA Ops:
  6.5 648.6 %copy-start = (bf16[144,288]{1,0:T(8,128)(2,1)S(1)}, bf16[144,288]{1,0:T(8,128)(2,1)}, u32[]{:S(2)}) copy-start(bf16[144,288]{1,0:T(8,128)(2,1)} %param.25) | copy-start | bytes 248836
  6.5 189.0 %all-reduce.9.cloned.1.call-start = ((), (), s32[]{:S(2)}) async-start(), calls=%async_computation.5 | async-start | bytes 524288 | tf_op jit(solution)/shard_map/psum | solution.py:106
  79.1 1.8 copy-start.8
  80.9 3.3 copy-start.6
  198.0 21.1 %all-to-all-start = ((f32[32,1,2048]{2,1,0:T(1,128)}), f32[32,1,2048]{2,1,0:T(1,128)S(1)}, u32[]{:S(2)}, u32[]{:S(2)}) async-start(f32[32,1,2048]{2,1,0:T(1,128)} %reshape.614), calls=%async_computation | async-start | bytes 524288 | tf_op jit(solution)/shard_map/all_to_all | solution.py:110
  208.5 2.1 copy-start.7
  273.5 126.9 %all-to-all-start.2 = ((bf16[32,2,512]{2,1,0:T(2,128)(2,1)}), bf16[32,2,512]{2,1,0:T(2,128)(2,1)S(1)}, u32[]{:S(2)}, u32[]{:S(2)}) async-start(bf16[32,2,512]{2,1,0:T(2,128)(2,1)} %reshape.616), calls=%async_computation.2 | async-start | bytes 131072 | tf_op jit(solution)/shard_map/all_to_all | solution.py:112
  277.3 121.0 %all-reduce.15.cloned.1.call-start = ((), (), s32[]{:S(2)}) async-start(), calls=%async_computation.9 | async-start | bytes 786432 | tf_op jit(solution)/shard_map/psum | solution.py:171
  400.4 19.3 %all-to-all-start.1 = ((f32[32,1,1024]{2,1,0:T(1,128)}), f32[32,1,1024]{2,1,0:T(1,128)S(1)}, u32[]{:S(2)}, u32[]{:S(2)}) async-start(f32[32,1,1024]{2,1,0:T(1,128)} %reshape.618), calls=%async_computation.1 | async-start | bytes 262144 | tf_op jit(solution)/shard_map/all_to_all | solution.py:111
  410.3 189.0 %all-reduce.11.cloned.1.call-start = ((), (), s32[]{:S(2)}) async-start(), calls=%async_computation.6 | async-start | bytes 2097152 | tf_op jit(solution)/shard_map/psum | solution.py:186
  421.3 2.0 copy-start.9
  440.0 4.6 copy-start.5
  442.5 3.5 copy-start.2
  445.9 276.8 %reduce-scatter.2.cloned.1.call-start = ((), (), s32[]{:S(2)}) async-start(), calls=%async_computation.7 | async-start | bytes 2785280 | tf_op jit(solution)/shard_map/reduce_scatter | solution.py:208
  630.5 23.8 %copy-start.1 = (f32[256,4,144]{2,0,1:T(8,128)}, f32[256,4,144]{2,0,1:T(8,128)S(1)}, u32[]{:S(2)}) copy-start(f32[256,4,144]{2,0,1:T(8,128)S(1)} %get-tuple-element.13) | copy-start | bytes 1769476
  654.3 1.1 copy-start.3
  664.9 77.9 %copy-start.4 = (bf16[288,144]{0,1:T(8,128)(2,1)S(1)}, bf16[288,144]{0,1:T(8,128)(2,1)}, u32[]{:S(2)}) copy-start(bf16[288,144]{0,1:T(8,128)(2,1)} %param.27) | copy-start | bytes 248836
  664.9 235.2 %all-reduce.13.cloned.1.call-start = ((), (), s32[]{:S(2)}) async-start(), calls=%async_computation.8 | async-start | bytes 2097152
Sparse Core Ops, SparseCore 0:
  76.6 118.8 all-reduce.8
  280.7 117.4 all-reduce.14
  446.0 153.2 all-reduce.10
  665.0 57.6 reduce-scatter.1
  745.1 154.9 all-reduce.12
where the time goes:
time: 938 us; the launch traced here: 937 us
  waiting for transfers between devices  574 us (61%)
  blocking collectives  262 us (28%)
  local copies, waits for them, and re-layouts  38.9 us (4%)
  starting transfers between devices  24 us (3%)
  between operations  15 us (2%)
  other arithmetic  14.8 us (2%)
    unnamed x6, waiting for transfers between devices  154 us
    psum x1, waiting for transfers between devices, body(): total_num, total_den = lax.psum((group_num, group_den), 'gx')  120 us
    psum x1, waiting for transfers between devices, body(): attn_full = lax.psum(attn_part, 'gy')  116 us
    psum x1, waiting for transfers between devices, body(): lax.psum((project(w_query), project(w_key), project(w_value)), 'gx')  111 us
    reduce_scatter x1, waiting for transfers between devices, body(): lax.psum_scatter(gate_and_up.reshape(ff_input.shape[0], steps_count, 2 *...  57.8 us
    psum x1, blocking collectives, body(): lax.psum((project(w_query), project(w_key), project(w_value)), 'gx')  47.4 us
    all_gather x1, blocking collectives, body(): lax.all_gather(inputs, 'gy', axis=0, tiled=True).astype(jnp.float32)  37.6 us
    all_gather x1, blocking collectives, body(): normed = lax.all_gather(normed_share, 'gy', axis=0, tiled=True)  36.1 us
  transfers between devices with their start and end apart: 8, of which 7 were waited for; matrix products, arithmetic and copies ran while one was open for 2% of the time, Pallas kernels for 0%

commit v1 on v0

--- a/solution.py
+++ b/solution.py
@@ -107,7 +107,12 @@
         (project(w_query), project(w_key), project(w_value)), "gx"
     )
     query_raw, key_raw, value_raw = (
-        lax.all_to_all(query_sum, "gy", split_axis=0, concat_axis=2, tiled=True),
+        jnp.concatenate(
+            lax.all_to_all(
+                jnp.stack(jnp.split(query_sum, lax.axis_size("gy"), axis=0)), "gy", 0, 0
+            ),
+            axis=2,
+        ),
         lax.all_to_all(key_sum, "gy", split_axis=0, concat_axis=2, tiled=True),
         lax.all_to_all(value_sum, "gy", split_axis=0, concat_axis=2, tiled=True),
     )

time: 938 us -> 971 us (1.035)
  local copies, waits for them, and re-layouts: 38.9 us -> 73.6 us
    another operation x1 -> x37, local copies, waits for them, and re-layouts: 0.16 us -> 29.8 us  [the longest x35 29.4 us: body(): jnp.stack(jnp.split(query_sum, lax.axis_size('gy'), axis=0))]
where the time goes in v1:
time: 971 us; the launch traced here: 969 us
  waiting for transfers between devices  568 us (58%)
  blocking collectives  262 us (27%)
  local copies, waits for them, and re-layouts  73.6 us (8%)
  starting transfers between devices  24 us (2%)
  other arithmetic  17.9 us (2%)
  between operations  15.4 us (2%)
    unnamed x6, waiting for transfers between devices  154 us
    psum x1, waiting for transfers between devices, body(): total_num, total_den = lax.psum((group_num, group_den), 'gx')  120 us
    psum x1, waiting for transfers between devices, body(): attn_full = lax.psum(attn_part, 'gy')  116 us
    psum x1, waiting for transfers between devices, body(): lax.psum((project(w_query), project(w_key), project(w_value)), 'gx')  106 us
    reduce_scatter x1, waiting for transfers between devices, body(): lax.psum_scatter(gate_and_up.reshape(ff_input.shape[0], steps_count, 2 *...  57.8 us
    psum x1, blocking collectives, body(): lax.psum((project(w_query), project(w_key), project(w_value)), 'gx')  47.3 us
    all_gather x1, blocking collectives, body(): lax.all_gather(inputs, 'gy', axis=0, tiled=True).astype(jnp.float32)  37.7 us
    all_gather x1, blocking collectives, body(): normed = lax.all_gather(normed_share, 'gy', axis=0, tiled=True)  36.1 us
  transfers between devices with their start and end apart: 8, of which 7 were waited for; matrix products, arithmetic and copies ran while one was open for 2% of the time, Pallas kernels for 0%

profile of v1, /device:TPU:1, one launch (start us, length us, event | category | flops | bytes accessed | tf_op | source)
XLA Modules:
  0.0 969.3 jit_solution(12792648736020877722)
XLA Ops:
  8.7 29.8 %psum.70 = f32[8,4]{0,1:T(4,128)S(1)} all-reduce(f32[8,4]{0,1:T(4,128)S(1)} %fusion.33), channel_id=1, replica_groups=mesh['gx'=16,'gy'=32] {'gx'}, use_global_device_ids=true, to_apply=%region_3.0 | all-reduce | flops 32 | bytes 256 | tf_op jit(solution)/shard_map/psum | solution.py:93
  39.2 36.1 %all_gather.10 = bf16[256,4,144]{2,0,1:T(8,128)(2,1)S(1)} all-gather(bf16[8,4,144]{2,0,1:T(8,128)(2,1)S(1)} %fusion.35), channel_id=1, replica_groups=mesh['gx'=16,'gy'=32] {'gy'}, dimensions={0}, use_global_device_ids=true | all-gather | bytes 304128 | tf_op jit(solution)/shard_map/all_gather | solution.py:97
  75.3 1.8 fusion.37
  80.2 2.8 fusion.65
  89.9 106.2 %all-reduce.9.cloned.1.call-done = f32[256,4,64]{0,2,1:T(8,128)} async-done(((f32[256,4,64]{0,2,1:T(8,128)}), f32[256,4,64]{0,2,1:T(8,128)}) %all-reduce.9.cloned.1.call-update) | async-done | bytes 262160 | tf_op jit(solution)/shard_map/psum | solution.py:106
  196.2 3.4 slice_bitcast_fusion.19
  199.7 1.6 copy.323
  201.3 1.6 copy.324
  202.9 1.6 copy.325
  204.5 1.6 copy.326
  206.1 1.6 copy.327
  208.2 1.9 slice_bitcast_fusion
  210.1 1.6 copy.335
  211.8 1.6 copy.336
  213.3 1.6 copy.337
  214.9 1.6 copy.338
  216.5 1.6 copy.339
  230.6 9.9 %all-to-all-start = ((f32[32,1,2048]{2,1,0:T(1,128)}), f32[32,1,2048]{2,1,0:T(1,128)S(1)}, u32[]{:S(2)}, u32[]{:S(2)}) async-start(f32[32,1,2048]{2,1,0:T(1,128)} %reshape.613), calls=%async_computation | async-start | bytes 524288 | tf_op jit(solution)/shard_map/all_to_all | solution.py:111
  241.2 2.3 copy.401
  245.2 6.6 all-to-all-done
  252.2 1.3 reduce.5
  257.0 47.3 %all-reduce.16 = (bf16[256,4,32]{0,2,1:T(8,128)(2,1)S(1)}, f32[8,4,4,2]{0,2,3,1:T(4,128)S(1)}) all-reduce(f32[256,4,32]{0,2,1:T(8,128)S(1)} %copy-done.4, f32[8,4,4,2]{0,2,3,1:T(4,128)S(1)} %copy.371), channel_id=1, replica_groups=mesh['gx'=16,'gy'=32] {'gx'}, use_global_device_ids=true, to_apply=%region_8.10 | all-reduce | flops 33024 | bytes 198656 | tf_op jit(solution)/shard_map/psum | solution.py:106
  305.4 3.8 all-to-all-start.2
  310.0 120.2 %all-reduce.15.cloned.1.call-done = (f32[8,4,4,2,256]{4,3,2,1,0:T(2,128)}, f32[256,4,32]{0,2,1:T(8,128)}) async-done(((f32[8,4,4,2,256]{4,3,2,1,0:T(2,128)}, f32[256,4,32]{0,2,1:T(8,128)}), (f32[8,4,4,2,256]{4,3,2,1,0:T(2,128)}, f32[256,4,32]{0,2,1:T(8,128)})) %all-reduce.15.cloned.1.call-update) | async-done | bytes 393232 | tf_op jit(solution)/shard_map/psum | solution.py:176
  432.3 9.9 %all-to-all-start.1 = ((f32[32,1,1024]{2,1,0:T(1,128)}), f32[32,1,1024]{2,1,0:T(1,128)S(1)}, u32[]{:S(2)}, u32[]{:S(2)}) async-start(f32[32,1,1024]{2,1,0:T(1,128)} %reshape.617), calls=%async_computation.1 | async-start | bytes 262144 | tf_op jit(solution)/shard_map/all_to_all | solution.py:116
  444.1 7.4 all-to-all-done.1
  455.6 1.3 copy.398
  456.9 2.3 reshape.619
  459.2 12.7 %all_to_all.44 = bf16[32,2,1024]{2,1,0:T(2,128)(2,1)S(1)} all-to-all(bf16[32,2,1024]{2,1,0:T(2,128)(2,1)S(1)} %reshape.619), channel_id=1, replica_groups=mesh['gx'=16,'gy'=32] {'gy'}, dimensions={0} | all-to-all | bytes 262144 | tf_op jit(solution)/shard_map/all_to_all | solution.py:186
  471.9 2.4 reshape.620
  474.4 2.1 copy.400
  476.5 1.3 fusion.16
  477.9 37.7 %all_gather.9 = bf16[256,4,144]{2,1,0:T(4,128)(2,1)S(1)} all-gather(bf16[8,4,144]{2,1,0:T(4,128)(2,1)S(1)} %copy-done.5), channel_id=1, replica_groups=mesh['gx'=16,'gy'=32] {'gy'}, dimensions={0}, use_global_device_ids=true | all-gather | bytes 304128 | tf_op jit(solution)/shard_map/all_gather | solution.py:192
  515.5 115.8 %all-reduce.11.cloned.1.call-done = f32[256,4,144]{2,0,1:T(8,128)} async-done(((f32[256,4,144]{2,0,1:T(8,128)}), f32[256,4,144]{2,0,1:T(8,128)}) %all-reduce.11.cloned.1.call-update) | async-done | bytes 589840 | tf_op jit(solution)/shard_map/psum | solution.py:191
  631.3 1.4 multiply_reduce_fusion.1
  632.8 28.1 %psum.77 = f32[256,4]{0,1:T(4,128)S(1)} all-reduce(f32[256,4]{0,1:T(4,128)S(1)} %multiply_reduce_fusion.1), channel_id=1, replica_groups=mesh['gx'=16,'gy'=32] {'gx'}, use_global_device_ids=true, to_apply=%region_15.17 | all-reduce | flops 1024 | bytes 8192 | tf_op jit(solution)/shard_map/psum | solution.py:193
  660.9 1.6 multiply_reduce_fusion
  662.5 23.6 %psum.78 = f32[256,4]{0,1:T(4,128)S(1)} all-reduce(f32[256,4]{0,1:T(4,128)S(1)} %get-tuple-element.12), channel_id=1, replica_groups=mesh['gx'=16,'gy'=32] {'gx'}, use_global_device_ids=true, to_apply=%region_17.19 | all-reduce | flops 1024 | bytes 8192 | tf_op jit(solution)/shard_map/psum | solution.py:197
  687.8 1.6 pad_maximum_fusion
  689.4 2.1 copy.380
  691.5 1.9 reshape.524
  693.4 3.4 copy.381
  696.9 57.8 %reduce-scatter.2.cloned.1.call-done = f32[16,4,576]{2,0,1:T(8,128)} async-done(((f32[256,4,576]{2,0,1:T(8,128)}), f32[16,4,576]{2,0,1:T(8,128)}) %reduce-scatter.2.cloned.1.call-update) | async-done | bytes 147472 | tf_op jit(solution)/shard_map/reduce_scatter | solution.py:213
  755.8 19.0 %all_gather.11 = bf16[256,4,288]{2,0,1:T(8,128)(2,1)S(1)} all-gather(bf16[16,4,288]{2,0,1:T(8,128)(2,1)S(1)} %fusion.31), channel_id=1, replica_groups=mesh['gx'=16,'gy'=32] {'gx'}, dimensions={0}, use_global_device_ids=true | all-gather | bytes 626688 | tf_op jit(solution)/shard_map/all_gather | solution.py:223
  775.2 1.7 copy.382
  776.9 1.3 dynamic-slice
  778.8 153.4 %all-reduce.13.cloned.1.call-done = f32[256,4,144]{2,1,0:T(4,128)} async-done(((f32[256,4,144]{2,1,0:T(4,128)}), f32[256,4,144]{2,1,0:T(4,128)}) %all-reduce.13.cloned.1.call-update) | async-done | bytes 589840
  933.2 28.1 %psum.79 = f32[8,4]{0,1:T(4,128)S(1)} all-reduce(f32[8,4]{0,1:T(4,128)S(1)} %copy.383), channel_id=1, replica_groups=mesh['gx'=16,'gy'=32] {'gx'}, use_global_device_ids=true, to_apply=%region_21.23 | all-reduce | flops 32 | bytes 256 | tf_op jit(solution)/shard_map/psum | solution.py:228
  (213 shorter events, 46.8 us)
Async XLA Ops:
  6.5 680.5 %copy-start = (bf16[144,288]{1,0:T(8,128)(2,1)S(1)}, bf16[144,288]{1,0:T(8,128)(2,1)}, u32[]{:S(2)}) copy-start(bf16[144,288]{1,0:T(8,128)(2,1)} %param.25) | copy-start | bytes 248836
  6.5 189.6 %all-reduce.9.cloned.1.call-start = ((), (), s32[]{:S(2)}) async-start(), calls=%async_computation.5 | async-start | bytes 524288 | tf_op jit(solution)/shard_map/psum | solution.py:106
  80.2 2.8 copy-start.22
  83.0 4.9 copy-start.14
  85.5 114.1 %copy-start.20 = (s32[8]{0:T(128)}, s32[8]{0:T(128)S(1)}, u32[]{:S(2)}) copy-start(s32[8]{0:T(128)S(1)} %get-tuple-element.15) | copy-start | bytes 100
  196.2 12.1 %copy-start.1 = (f32[256,4,64]{0,2,1:T(8,128)S(1)}, f32[256,4,64]{0,2,1:T(8,128)}, u32[]{:S(2)}) copy-start(f32[256,4,64]{0,2,1:T(8,128)} %all-reduce.9.cloned.1.call-done) | copy-start | bytes 786436
  210.1 15.5 %copy-start.11 = (f32[1,8,4,64]{3,1,2,0:T(8,128)S(1)}, f32[1,8,4,64]{3,1,2,0:T(8,128)}, u32[]{:S(2)}) copy-start(f32[1,8,4,64]{3,1,2,0:T(8,128)} %copy.323) | copy-start | bytes 24580
  210.1 15.5 %copy-start.12 = (f32[1,8,4,64]{3,1,2,0:T(8,128)S(1)}, f32[1,8,4,64]{3,1,2,0:T(8,128)}, u32[]{:S(2)}) copy-start(f32[1,8,4,64]{3,1,2,0:T(8,128)} %copy.324) | copy-start | bytes 24580
  210.1 15.6 %copy-start.10 = (f32[1,8,4,64]{3,1,2,0:T(8,128)S(1)}, f32[1,8,4,64]{3,1,2,0:T(8,128)}, u32[]{:S(2)}) copy-start(f32[1,8,4,64]{3,1,2,0:T(8,128)} %copy.325) | copy-start | bytes 24580
  210.1 15.6 %copy-start.9 = (f32[1,8,4,64]{3,1,2,0:T(8,128)S(1)}, f32[1,8,4,64]{3,1,2,0:T(8,128)}, u32[]{:S(2)}) copy-start(f32[1,8,4,64]{3,1,2,0:T(8,128)} %copy.326) | copy-start | bytes 24580
  210.1 15.6 %copy-start.8 = (f32[1,8,4,64]{3,1,2,0:T(8,128)S(1)}, f32[1,8,4,64]{3,1,2,0:T(8,128)}, u32[]{:S(2)}) copy-start(f32[1,8,4,64]{3,1,2,0:T(8,128)} %copy.327) | copy-start | bytes 24580
  230.6 21.1 %all-to-all-start = ((f32[32,1,2048]{2,1,0:T(1,128)}), f32[32,1,2048]{2,1,0:T(1,128)S(1)}, u32[]{:S(2)}, u32[]{:S(2)}) async-start(f32[32,1,2048]{2,1,0:T(1,128)} %reshape.613), calls=%async_computation | async-start | bytes 524288 | tf_op jit(solution)/shard_map/all_to_all | solution.py:111
  241.2 2.9 copy-start.18
  241.2 3.1 copy-start.15
  253.7 1.2 copy-start.3
  253.7 1.2 copy-start.19
  255.0 2.0 copy-start.4
  256.0 186.5 %copy-start.21 = (s32[8]{0:T(128)S(1)}, s32[8]{0:T(128)}, u32[]{:S(2)}) copy-start(s32[8]{0:T(128)} %copy-done.20) | copy-start | bytes 100
  256.0 186.5 %copy-start.23 = (s32[1,8]{1,0:T(1,128)S(1)}, s32[1,8]{1,0:T(1,128)}, u32[]{:S(2)}) copy-start(s32[1,8]{1,0:T(1,128)} %get-tuple-element.69) | copy-start | bytes 100
  256.0 186.5 %copy-start.24 = (s32[1,8]{1,0:T(1,128)S(1)}, s32[1,8]{1,0:T(1,128)}, u32[]{:S(2)}) copy-start(s32[1,8]{1,0:T(1,128)} %get-tuple-element.67) | copy-start | bytes 100
  256.0 186.5 %copy-start.25 = (s32[1,8]{1,0:T(1,128)S(1)}, s32[1,8]{1,0:T(1,128)}, u32[]{:S(2)}) copy-start(s32[1,8]{1,0:T(1,128)} %fusion.59) | copy-start | bytes 100
  256.0 186.5 %copy-start.26 = (s32[1,8]{1,0:T(1,128)S(1)}, s32[1,8]{1,0:T(1,128)}, u32[]{:S(2)}) copy-start(s32[1,8]{1,0:T(1,128)} %fusion.58) | copy-start | bytes 100
  305.4 126.9 %all-to-all-start.2 = ((bf16[32,2,512]{2,1,0:T(2,128)(2,1)}), bf16[32,2,512]{2,1,0:T(2,128)(2,1)S(1)}, u32[]{:S(2)}, u32[]{:S(2)}) async-start(bf16[32,2,512]{2,1,0:T(2,128)(2,1)} %reshape.615), calls=%async_computation.2 | async-start | bytes 131072 | tf_op jit(solution)/shard_map/all_to_all | solution.py:117
  309.2 120.9 %all-reduce.15.cloned.1.call-start = ((), (), s32[]{:S(2)}) async-start(), calls=%async_computation.9 | async-start | bytes 786432 | tf_op jit(solution)/shard_map/psum | solution.py:176
  432.3 19.3 %all-to-all-start.1 = ((f32[32,1,1024]{2,1,0:T(1,128)}), f32[32,1,1024]{2,1,0:T(1,128)S(1)}, u32[]{:S(2)}, u32[]{:S(2)}) async-start(f32[32,1,1024]{2,1,0:T(1,128)} %reshape.617), calls=%async_computation.1 | async-start | bytes 262144 | tf_op jit(solution)/shard_map/all_to_all | solution.py:116
  442.2 189.1 %all-reduce.11.cloned.1.call-start = ((), (), s32[]{:S(2)}) async-start(), calls=%async_computation.6 | async-start | bytes 2097152 | tf_op jit(solution)/shard_map/psum | solution.py:191
  453.2 2.0 copy-start.27
  471.9 4.6 copy-start.13
  474.3 3.5 copy-start.5
  476.5 184.4 %copy-start.16 = (f32[1,144]{1,0:T(1,128)S(1)}, f32[1,144]{1,0:T(1,128)}, u32[]{:S(2)}) copy-start(f32[1,144]{1,0:T(1,128)} %get-tuple-element.56) | copy-start | bytes 1732
  477.8 208.3 %copy-start.17 = (f32[1,144]{1,0:T(1,128)S(1)}, f32[1,144]{1,0:T(1,128)}, u32[]{:S(2)}) copy-start(f32[1,144]{1,0:T(1,128)} %get-tuple-element.55) | copy-start | bytes 1732
  477.8 276.9 %reduce-scatter.2.cloned.1.call-start = ((), (), s32[]{:S(2)}) async-start(), calls=%async_computation.7 | async-start | bytes 2785280 | tf_op jit(solution)/shard_map/reduce_scatter | solution.py:213
  662.5 23.8 %copy-start.2 = (f32[256,4,144]{2,0,1:T(8,128)}, f32[256,4,144]{2,0,1:T(8,128)S(1)}, u32[]{:S(2)}) copy-start(f32[256,4,144]{2,0,1:T(8,128)S(1)} %get-tuple-element.13) | copy-start | bytes 1769476
  686.3 1.1 copy-start.6
  696.8 77.9 %copy-start.7 = (bf16[288,144]{0,1:T(8,128)(2,1)S(1)}, bf16[288,144]{0,1:T(8,128)(2,1)}, u32[]{:S(2)}) copy-start(bf16[288,144]{0,1:T(8,128)(2,1)} %param.27) | copy-start | bytes 248836
  696.9 235.4 %all-reduce.13.cloned.1.call-start = ((), (), s32[]{:S(2)}) async-start(), calls=%async_computation.8 | async-start | bytes 2097152
Sparse Core Ops, SparseCore 0:
  77.2 118.8 all-reduce.8
  312.7 117.4 all-reduce.14
  477.9 153.3 all-reduce.10
  697.0 57.6 reduce-scatter.1
  777.0 155.1 all-reduce.12
